TPU v7x, 32 devices: a whole 2x2x4 slice. The times are simulated.
32 devices in a mesh: fiber: 8 (over z, core), group: 4 (over y, x).
Axes of the slice: x: 2, y: 2, z: 4, core: 2. Of those that a mesh axis runs over, the one named last changes fastest.
Arguments:
- field_slab: float32 [512, 64, 2048], P('fiber', 'group'), may hold values from -42 to 42
- start_basis: float32 [512, 128], replicated, may hold values from -6 to 6
Outputs:
- factor: float32 [512, 128], replicated
- core_slab: float32 [128, 64, 2048], P(None, 'group', 'fiber')
All inputs are finite; a program needn't handle non-finite values.
Results may differ from a plain program's by a relative error of at most 0.0003.
Values sent between devices are 32-bit elements; how exact they have to be, the bound alone decides.
No kernel may reach another device: no remote copies, remote signals or barrier semaphores. Data moves between devices by JAX's collectives and lax.ppermute only.
A program may use at most 128 MiB of HBM per device.

v0:
```python
import jax
import jax.numpy as jnp
from jax import lax
from jax.sharding import PartitionSpec as P

ITERS = 2
precise = lax.Precision.HIGHEST


def orthonormal(images):
    inner_products = jnp.dot(images.T, images, precision=precise)
    cholesky_factor = jnp.linalg.cholesky(inner_products)
    return lax.linalg.triangular_solve(
        cholesky_factor, images, left_side=False, lower=True, transpose_a=True
    )


def on_device(field_slab, start_basis):
    column_count = field_slab.shape[1] * field_slab.shape[2] * lax.axis_size("group")
    regrouped = lax.all_to_all(field_slab, "fiber", split_axis=2, concat_axis=0, tiled=True)
    columns = regrouped.reshape(regrouped.shape[0], regrouped.shape[1] * regrouped.shape[2])
    local_gram = jnp.dot(columns, columns.T, precision=precise)
    subspace = start_basis
    fiber_share = lax.psum_scatter(local_gram, "fiber", scatter_dimension=0, tiled=True)
    gram_share = lax.psum(fiber_share, "group") / column_count
    for iteration in range(ITERS):
        image_rows = jnp.dot(gram_share, subspace, precision=precise)
        subspace = orthonormal(lax.all_gather(image_rows, "fiber", axis=0, tiled=True))
    core_slab = jnp.einsum("mk,mbc->kbc", subspace, regrouped, precision=precise)
    return (subspace, core_slab)


def solution(mesh):
    return jax.shard_map(
        on_device,
        mesh=mesh,
        in_specs=(P("fiber", "group", None), P()),
        out_specs=(P(), P(None, "group", "fiber")),
        check_vma=False,
    )
```

profile of v0, /device:TPU:0, one launch (start us, length us, event | category | flops | bytes accessed | tf_op | source)
XLA Modules:
  0.0 485.6 jit_solution(11098625435497381214)
XLA Ops:
  7.2 0.0 copy-start
  7.2 0.0 reduce-scatter.2.cloned.1.call-start
  7.2 15.6 %copy.22 = f32[64,16,2048]{0,1,2:T(8,128)} copy(f32[64,16,2048]{2,1,0:T(8,128)} %param.5) | data formatting | bytes 16777216 | tf_op args[0]
  22.8 15.4 %reshape.27 = f32[8,1,262144]{2,1,0:T(1,128)} reshape(f32[2048,16,64]{2,1,0:T(8,128)} %bitcast.49) | data formatting | bytes 16777216
  38.2 190.7 %all_to_all.18 = f32[8,1,262144]{2,1,0:T(1,128)} all-to-all(f32[8,1,262144]{2,1,0:T(1,128)} %reshape.27), channel_id=1, replica_groups=mesh['fiber'=8,'group'=4] {'fiber'}, dimensions={0} | all-to-all | bytes 16777216 | tf_op jit(solution)/shard_map/all_to_all | solution.py:20
  228.9 0.5 broadcast.36
  229.4 26.2 %reduce.4 = f32[8,262144]{1,0:T(8,128)} reduce(f32[8,1,262144]{2,1,0:T(1,128)} %all_to_all.18, f32[]{:T(128)} %broadcast.36), dimensions={1}, to_apply=%all_to_all.13.reduce_sub_computation | reduce | bytes 16777220 | tf_op jit(solution)/shard_map/all_to_all | solution.py:20
  255.7 15.6 %reshape.28 = f32[2048,16,64]{2,1,0:T(8,128)} reshape(f32[8,262144]{1,0:T(8,128)} %reduce.4) | data formatting | bytes 16777216
  271.3 15.8 %copy.23 = f32[64,16,8,256]{3,1,0,2:T(8,128)} copy(f32[64,16,8,256]{0,1,3,2:T(8,128)} %bitcast.47) | data formatting | bytes 16777216 | tf_op jit(solution)/shard_map/all_to_all | solution.py:20
  287.0 11.5 %copy.30 = f32[64,8,16,256]{3,1,2,0:T(8,128)S(1)} copy(f32[64,8,16,256]{3,2,1,0:T(8,128)} %bitcast.51) | data formatting | bytes 16777216
  298.5 14.9 %fusion.19 = f32[512,512]{1,0:T(8,128)} fusion(f32[512,4096]{1,0:T(8,128)S(1)} %bitcast.46), kind=kOutput, calls=%fused_computation.29 | convolution fusion | flops 12884901888 | bytes 9437184 | tf_op jit(solution)/shard_map/dot_general | solution.py:22
  313.5 0.0 reduce-scatter.2.cloned.1.call-update
  313.5 0.0 all-reduce.2.cloned.1.call-start
  313.5 32.2 %reduce-scatter.2.cloned.1.call-done = f32[64,512]{1,0:T(8,128)} async-done(((f32[512,512]{1,0:T(8,128)}), f32[64,512]{1,0:T(8,128)}) %reduce-scatter.2.cloned.1.call-update) | async-done | bytes 131088 | tf_op jit(solution)/shard_map/reduce_scatter | solution.py:24
  345.7 0.0 all-reduce.2.cloned.1.call-update
  345.7 12.8 %copy.26 = f32[8,64,16,256]{3,1,0,2:T(8,128)} copy(f32[8,64,16,256]{1,2,3,0:T(8,128)} %bitcast.48) | data formatting | bytes 16777216 | tf_op jit(solution)/shard_map/all_to_all | solution.py:20
  358.5 30.5 %all-reduce.2.cloned.1.call-done = f32[64,512]{1,0:T(8,128)} async-done(((f32[64,512]{1,0:T(8,128)}), f32[64,512]{1,0:T(8,128)}) %all-reduce.2.cloned.1.call-update) | async-done | bytes 131088 | tf_op jit(solution)/shard_map/psum | solution.py:25
  389.0 0.0 copy-done
  389.0 1.2 fusion.4
  390.2 14.3 %all_gather.6 = f32[512,128]{1,0:T(8,128)S(1)} all-gather(f32[64,128]{1,0:T(8,128)S(1)} %fusion.4), channel_id=1, replica_groups=mesh['fiber'=8,'group'=4] {'fiber'}, dimensions={0}, use_global_device_ids=true | all-gather | bytes 294912 | tf_op jit(solution)/shard_map/all_gather | solution.py:28
  404.5 0.6 fusion.20
  405.1 0.1 copy.24
  405.2 11.7 %cholesky.44 = f32[128,128]{1,0:T(8,128)S(1)} custom-call(f32[128,128]{1,0:T(8,128)S(1)} %fusion.12), custom_call_target="Cholesky" | custom-call | tf_op jit(solution)/shard_map/jit(cholesky)/cholesky | solution.py:12
  416.9 0.6 compare_reduce_fusion.1
  417.6 0.7 fusion.6
  418.2 9.8 %custom-call.6 = f32[1,128,128]{1,2,0:T(8,128)S(1)} custom-call(f32[1,128,128]{2,1,0:T(8,128)S(1)} %fusion.6), custom_call_target="InvertDiagBlocksLowerTriangular" | custom-call | tf_op jit(solution)/shard_map/triangular_solve/custom-call.0 | solution.py:13
  428.0 0.4 convolution_bitcast_fusion
  428.5 1.3 fusion.2
  429.8 14.4 %all_gather.7 = f32[512,128]{1,0:T(8,128)S(1)} all-gather(f32[64,128]{1,0:T(8,128)S(1)} %fusion.2), channel_id=1, replica_groups=mesh['fiber'=8,'group'=4] {'fiber'}, dimensions={0}, use_global_device_ids=true | all-gather | bytes 294912 | tf_op jit(solution)/shard_map/all_gather | solution.py:28
  444.2 0.6 fusion.21
  444.8 0.1 copy.25
  444.9 11.7 %cholesky.55 = f32[128,128]{1,0:T(8,128)S(1)} custom-call(f32[128,128]{1,0:T(8,128)S(1)} %fusion.10), custom_call_target="Cholesky" | custom-call | tf_op jit(solution)/shard_map/jit(cholesky)/cholesky | solution.py:12
  456.7 0.6 compare_reduce_fusion
  457.3 0.7 fusion.7
  458.0 9.8 %custom-call.7 = f32[1,128,128]{1,2,0:T(8,128)S(1)} custom-call(f32[1,128,128]{2,1,0:T(8,128)S(1)} %fusion.7), custom_call_target="InvertDiagBlocksLowerTriangular" | custom-call | tf_op jit(solution)/shard_map/triangular_solve/custom-call.0 | solution.py:13
  467.8 0.4 fusion.8
  468.2 0.8 copy.27
  469.1 6.9 %fusion = f32[128,16,256]{2,0,1:T(8,128)S(1)} fusion(f32[512,16,256]{2,0,1:T(8,128)} %bitcast.50, f32[128,512]{1,0:T(8,128)S(1)} %fusion.8), kind=kOutput, calls=%fused_computation.1 | convolution fusion | flops 3221225472 | bytes 10747904 | tf_op jit(solution)/shard_map/mk,mbc->kbc/dot_general | solution.py:29
  476.0 2.5 copy.28
  (4 shorter events, 0.1 us)
Async XLA Ops:
  7.2 381.9 %copy-start = (f32[512,128]{1,0:T(8,128)S(1)}, f32[512,128]{1,0:T(8,128)}, u32[]{:S(2)}) copy-start(f32[512,128]{1,0:T(8,128)} %param.6) | copy-start | bytes 786436
  7.2 338.5 %reduce-scatter.2.cloned.1.call-start = ((), (), s32[]{:S(2)}) async-start(), calls=%async_computation.2 | async-start | bytes 1179648 | tf_op jit(solution)/shard_map/reduce_scatter | solution.py:24
  313.5 75.5 %all-reduce.2.cloned.1.call-start = ((), (), s32[]{:S(2)}) async-start(), calls=%async_computation.3 | async-start | bytes 262144 | tf_op jit(solution)/shard_map/psum | solution.py:25
Sparse Core Ops, SparseCore 0:
  313.6 32.0 reduce-scatter.1
  348.6 40.4 all-reduce.1
where the time goes:
time: 489 us; the launch traced here: 486 us
  blocking collectives  219 us (45%)
  local copies, waits for them, and re-layouts  90.7 us (19%)
  other arithmetic  72 us (15%)
  waiting for transfers between devices  62.7 us (13%)
  matrix products  26.3 us (5%)
  between operations  14.4 us (3%)
    all_to_all x1, blocking collectives, on_device(): lax.all_to_all(field_slab, 'fiber', split_axis=2, concat_axis=0, tiled=True)  191 us
    unnamed x8, local copies, waits for them, and re-layouts  61.4 us
    reduce_scatter x1, waiting for transfers between devices, on_device(): lax.psum_scatter(local_gram, 'fiber', scatter_dimension=0, tiled=True)  32.2 us
    psum x1, waiting for transfers between devices, on_device(): gram_share = lax.psum(fiber_share, 'group') / column_count  30.5 us
    all_to_all x3, local copies, waits for them, and re-layouts, on_device(): lax.all_to_all(field_slab, 'fiber', split_axis=2, concat_axis=0, tiled=True)  29.1 us
    all_gather x2, blocking collectives, on_device(): lax.all_gather(image_rows, 'fiber', axis=0, tiled=True)  28.7 us
    all_to_all x1, other arithmetic, on_device(): lax.all_to_all(field_slab, 'fiber', split_axis=2, concat_axis=0, tiled=True)  26.2 us
    another operation x6, other arithmetic, orthonormal(): cholesky_factor = jnp.linalg.cholesky(inner_products)  24.8 us
  transfers between devices with their start and end apart: 2, of which 2 were waited for; matrix products, arithmetic and copies ran while one was open for 3% of the time, Pallas kernels for 0%

commit v1 on v0

--- a/solution.py
+++ b/solution.py
@@ -5,6 +5,12 @@
 
 ITERS = 2
 precise = lax.Precision.HIGHEST
+
+
+def summed_here(x, axis):
+    pieces = lax.all_gather(x, axis, axis=0, tiled=False)
+    summed = pieces.sum(axis=0)
+    return summed
 
 
 def orthonormal(images):
@@ -22,7 +28,7 @@
     local_gram = jnp.dot(columns, columns.T, precision=precise)
     subspace = start_basis
     fiber_share = lax.psum_scatter(local_gram, "fiber", scatter_dimension=0, tiled=True)
-    gram_share = lax.psum(fiber_share, "group") / column_count
+    gram_share = summed_here(fiber_share, "group") / column_count
     for iteration in range(ITERS):
         image_rows = jnp.dot(gram_share, subspace, precision=precise)
         subspace = orthonormal(lax.all_gather(image_rows, "fiber", axis=0, tiled=True))

time: 489 us -> 454 us (0.928)
  waiting for transfers between devices: 62.7 us -> 19.6 us
  blocking collectives: 219 us -> 230 us
    psum x1 -> x0, waiting for transfers between devices: 30.5 us -> none  [on_device(): gram_share = lax.psum(fiber_share, 'group') / column_count]
    reduce_scatter x1, waiting for transfers between devices: 32.2 us -> 19.5 us  [on_device(): lax.psum_scatter(local_gram, 'fiber', scatter_dimension=0, tiled=True)]
    all_gather x0 -> x1, blocking collectives: none -> 10.3 us  [summed_here(): pieces = lax.all_gather(x, axis, axis=0, tiled=False)]
  transfers between devices with their start and end apart: 2 -> 1, of which waited for: 2 -> 1; matrix products, arithmetic and copies ran while one was open for 3% -> 3% of each run, Pallas kernels for 0% -> 0%
where the time goes in v1:
time: 454 us; the launch traced here: 451 us
  blocking collectives  230 us (51%)
  local copies, waits for them, and re-layouts  90.3 us (20%)
  other arithmetic  72 us (16%)
  matrix products  24.4 us (5%)
  waiting for transfers between devices  19.6 us (4%)
  between operations  14.4 us (3%)
    all_to_all x1, blocking collectives, on_device(): lax.all_to_all(field_slab, 'fiber', split_axis=2, concat_axis=0, tiled=True)  191 us
    unnamed x8, local copies, waits for them, and re-layouts  61.4 us
    all_gather x2, blocking collectives, on_device(): lax.all_gather(image_rows, 'fiber', axis=0, tiled=True)  28.8 us
    all_to_all x3, local copies, waits for them, and re-layouts, on_device(): lax.all_to_all(field_slab, 'fiber', split_axis=2, concat_axis=0, tiled=True)  28.7 us
    all_to_all x1, other arithmetic, on_device(): lax.all_to_all(field_slab, 'fiber', split_axis=2, concat_axis=0, tiled=True)  26.2 us
    another operation x6, other arithmetic, orthonormal(): cholesky_factor = jnp.linalg.cholesky(inner_products)  24.8 us
    another operation x4, other arithmetic, orthonormal(): lax.linalg.triangular_solve(cholesky_factor, images, left_side=False, low...  20.9 us
    reduce_scatter x1, waiting for transfers between devices, on_device(): lax.psum_scatter(local_gram, 'fiber', scatter_dimension=0, tiled=True)  19.5 us
  transfers between devices with their start and end apart: 1, of which 1 were waited for; matrix products, arithmetic and copies ran while one was open for 3% of the time, Pallas kernels for 0%

profile of v1, /device:TPU:0, one launch (start us, length us, event | category | flops | bytes accessed | tf_op | source)
XLA Modules:
  0.0 450.7 jit_solution(11925346655807121087)
XLA Ops:
  7.2 0.0 copy-start
  7.2 0.0 reduce-scatter.2.cloned.1.call-start
  7.2 15.6 %copy.22 = f32[64,16,2048]{0,1,2:T(8,128)} copy(f32[64,16,2048]{2,1,0:T(8,128)} %param.5) | data formatting | bytes 16777216 | tf_op args[0]
  22.8 15.4 %reshape.28 = f32[8,1,262144]{2,1,0:T(1,128)} reshape(f32[2048,16,64]{2,1,0:T(8,128)} %bitcast.50) | data formatting | bytes 16777216
  38.2 190.9 %all_to_all.18 = f32[8,1,262144]{2,1,0:T(1,128)} all-to-all(f32[8,1,262144]{2,1,0:T(1,128)} %reshape.28), channel_id=1, replica_groups=mesh['fiber'=8,'group'=4] {'fiber'}, dimensions={0} | all-to-all | bytes 16777216 | tf_op jit(solution)/shard_map/all_to_all | solution.py:26
  229.1 0.5 broadcast.36
  229.6 26.2 %reduce.4 = f32[8,262144]{1,0:T(8,128)} reduce(f32[8,1,262144]{2,1,0:T(1,128)} %all_to_all.18, f32[]{:T(128)} %broadcast.36), dimensions={1}, to_apply=%all_to_all.13.reduce_sub_computation | reduce | bytes 16777220 | tf_op jit(solution)/shard_map/all_to_all | solution.py:26
  255.8 15.6 %reshape.29 = f32[2048,16,64]{2,1,0:T(8,128)} reshape(f32[8,262144]{1,0:T(8,128)} %reduce.4) | data formatting | bytes 16777216
  271.4 15.4 %copy.23 = f32[64,16,8,256]{3,1,0,2:T(8,128)} copy(f32[64,16,8,256]{0,1,3,2:T(8,128)} %bitcast.48) | data formatting | bytes 16777216 | tf_op jit(solution)/shard_map/all_to_all | solution.py:26
  286.9 11.5 %copy.30 = f32[64,8,16,256]{3,1,2,0:T(8,128)S(1)} copy(f32[64,8,16,256]{3,2,1,0:T(8,128)} %bitcast.52) | data formatting | bytes 16777216
  298.4 14.7 %fusion.19 = f32[512,512]{1,0:T(8,128)} fusion(f32[512,4096]{1,0:T(8,128)S(1)} %bitcast.47), kind=kOutput, calls=%fused_computation.29 | convolution fusion | flops 12884901888 | bytes 9437184 | tf_op jit(solution)/shard_map/dot_general | solution.py:28
  313.1 0.0 reduce-scatter.2.cloned.1.call-update
  313.1 12.8 %copy.26 = f32[8,64,16,256]{3,1,0,2:T(8,128)} copy(f32[8,64,16,256]{1,2,3,0:T(8,128)} %bitcast.49) | data formatting | bytes 16777216 | tf_op jit(solution)/shard_map/all_to_all | solution.py:26
  325.9 19.5 %reduce-scatter.2.cloned.1.call-done = f32[64,512]{1,0:T(8,128)} async-done(((f32[512,512]{1,0:T(8,128)}), f32[64,512]{1,0:T(8,128)}) %reduce-scatter.2.cloned.1.call-update) | async-done | bytes 131088 | tf_op jit(solution)/shard_map/reduce_scatter | solution.py:30
  345.4 10.3 %all-gather = f32[256,512]{1,0:T(8,128)S(1)} all-gather(f32[64,512]{1,0:T(8,128)} %reduce-scatter.2.cloned.1.call-done), channel_id=2, replica_groups=mesh['fiber'=8,'group'=4] {'group'}, dimensions={0}, use_global_device_ids=true | all-gather | bytes 655360 | tf_op jit(solution)/shard_map/all_gather | solution.py:11
  355.7 0.0 copy-done
  355.7 0.3 fusion.4
  356.0 14.4 %all_gather.14 = f32[512,128]{1,0:T(8,128)S(1)} all-gather(f32[64,128]{1,0:T(8,128)S(1)} %fusion.4), channel_id=1, replica_groups=mesh['fiber'=8,'group'=4] {'fiber'}, dimensions={0}, use_global_device_ids=true | all-gather | bytes 294912 | tf_op jit(solution)/shard_map/all_gather | solution.py:34
  370.4 0.6 fusion.20
  371.0 0.1 copy.24
  371.1 11.7 %cholesky.44 = f32[128,128]{1,0:T(8,128)S(1)} custom-call(f32[128,128]{1,0:T(8,128)S(1)} %fusion.12), custom_call_target="Cholesky" | custom-call | tf_op jit(solution)/shard_map/jit(cholesky)/cholesky | solution.py:18
  382.9 0.6 compare_reduce_fusion.1
  383.5 0.7 fusion.6
  384.2 9.8 %custom-call.6 = f32[1,128,128]{1,2,0:T(8,128)S(1)} custom-call(f32[1,128,128]{2,1,0:T(8,128)S(1)} %fusion.6), custom_call_target="InvertDiagBlocksLowerTriangular" | custom-call | tf_op jit(solution)/shard_map/triangular_solve/custom-call.0 | solution.py:19
  394.0 0.4 convolution_bitcast_fusion
  394.4 0.4 fusion.2
  394.8 14.4 %all_gather.15 = f32[512,128]{1,0:T(8,128)S(1)} all-gather(f32[64,128]{1,0:T(8,128)S(1)} %fusion.2), channel_id=1, replica_groups=mesh['fiber'=8,'group'=4] {'fiber'}, dimensions={0}, use_global_device_ids=true | all-gather | bytes 294912 | tf_op jit(solution)/shard_map/all_gather | solution.py:34
  409.3 0.6 fusion.21
  409.9 0.1 copy.25
  410.0 11.7 %cholesky.55 = f32[128,128]{1,0:T(8,128)S(1)} custom-call(f32[128,128]{1,0:T(8,128)S(1)} %fusion.10), custom_call_target="Cholesky" | custom-call | tf_op jit(solution)/shard_map/jit(cholesky)/cholesky | solution.py:18
  421.7 0.6 compare_reduce_fusion
  422.4 0.7 fusion.7
  423.0 9.8 %custom-call.7 = f32[1,128,128]{1,2,0:T(8,128)S(1)} custom-call(f32[1,128,128]{2,1,0:T(8,128)S(1)} %fusion.7), custom_call_target="InvertDiagBlocksLowerTriangular" | custom-call | tf_op jit(solution)/shard_map/triangular_solve/custom-call.0 | solution.py:19
  432.8 0.4 fusion.8
  433.3 0.8 copy.27
  434.1 6.9 %fusion = f32[128,16,256]{2,0,1:T(8,128)S(1)} fusion(f32[512,16,256]{2,0,1:T(8,128)} %bitcast.51, f32[128,512]{1,0:T(8,128)S(1)} %fusion.8), kind=kOutput, calls=%fused_computation.1 | convolution fusion | flops 3221225472 | bytes 10747904 | tf_op jit(solution)/shard_map/mk,mbc->kbc/dot_general | solution.py:35
  441.0 2.5 copy.28
  (5 shorter events, 0.1 us)
Async XLA Ops:
  7.2 348.6 %copy-start = (f32[512,128]{1,0:T(8,128)S(1)}, f32[512,128]{1,0:T(8,128)}, u32[]{:S(2)}) copy-start(f32[512,128]{1,0:T(8,128)} %param.6) | copy-start | bytes 786436
  7.2 338.2 %reduce-scatter.2.cloned.1.call-start = ((), (), s32[]{:S(2)}) async-start(), calls=%async_computation.2 | async-start | bytes 1179648 | tf_op jit(solution)/shard_map/reduce_scatter | solution.py:30
Sparse Core Ops, SparseCore 0:
  313.2 32.1 reduce-scatter.1
